TPU v7x, 512 devices: a whole 4x8x8 slice. The times are simulated.
512 devices in a mesh: lat: 16 (over x, z_hi, core), lon: 32 (over y, z_lo).
Axes of the slice: x: 4, y: 8, z: 8 (z_hi: 2, z_lo: 4; z = z_hi * 4 + z_lo), core: 2. Of those that a mesh axis runs over, the one named last changes fastest.
Arguments:
- inputs_below: bfloat16 [64, 128, 4096], P(None, 'lat', 'lon'), may hold values from -6 to 6
- hidden_prev: bfloat16 [64, 128, 4096], P(None, 'lat', 'lon'), may hold values from -0.8984375 to 0.8984375
- cell_prev: float32 [64, 128, 4096], P(None, 'lat', 'lon'), may hold values from -5 to 5
- kernel_weights: bfloat16 [9, 256, 128], replicated, may hold values from -0.1875 to 0.1875
- gate_bias: float32 [256], replicated, may hold values from -4 to 4
- readout: float32 [64], replicated, may hold values from -0.75 to 0.75
- target_field: float32 [128, 4096], P('lat', 'lon'), may hold values from -6 to 6
- land_mask: int32 [128, 4096], P('lat', 'lon'), may hold values 0 or 1
- fire_mask: int32 [128, 4096], P('lat', 'lon'), may hold values 0 or 1
- hidden_grad: bfloat16 [64, 128, 4096], P(None, 'lat', 'lon'), may hold values from -10 to 10
Outputs:
- hidden_next: bfloat16 [64, 128, 4096], P(None, 'lat', 'lon')
- cell_next: float32 [64, 128, 4096], P(None, 'lat', 'lon')
- grad_inputs: bfloat16 [64, 128, 4096], P(None, 'lat', 'lon')
- grad_hidden: bfloat16 [64, 128, 4096], P(None, 'lat', 'lon')
- grad_cell: float32 [64, 128, 4096], P(None, 'lat', 'lon')
- grad_kernel: float32 [9, 256, 128], replicated
- grad_bias: float32 [256], replicated
Inputs may be any that keep to these rules, and one draw needn't show every extreme that they name: `land_mask`: 1 marks land cells, 0 sea cells. `fire_mask`: 1 marks cells where fire danger is observed.
All inputs are finite; a program needn't handle non-finite values. No bound on the sum of `land_mask` or of `fire_mask` on one device may be relied on, other than what follows from the above.
Results may differ from a plain program's by a relative error of at most 0.0049.
Values may be sent and summed in bfloat16 or wider, within the bound.
A program may use at most 64 MiB of HBM per device.

v0:
```python
import math
import jax
import jax.numpy as jnp
from jax import lax
from jax.sharding import PartitionSpec as P


def with_halo(cells, sides, width, closed):
    for axis, dim in sides:
        count = lax.axis_size(axis)
        ends = count if closed else count - 1
        head = lax.slice_in_dim(cells, 0, width, axis=dim)
        tail = lax.slice_in_dim(cells, cells.shape[dim] - width, cells.shape[dim], axis=dim)
        cells = jnp.concatenate(
            [
                lax.ppermute(tail, axis, [(i, (i + 1) % count) for i in range(ends)]),
                cells,
                lax.ppermute(head, axis, [((i + 1) % count, i) for i in range(ends)]),
            ],
            axis=dim,
        )
    return cells


def shifted(value, axis, steps):
    count = lax.axis_size(axis)
    pairs = [(source, (source + steps) % count) for source in range(count)]
    return lax.ppermute(value, axis, pairs)


def extend(field):
    banded = with_halo(field, (("lat", 1),), 1, False)
    edge_rows = jnp.concatenate([field[:, :1], field[:, -1:]], axis=1)
    across = shifted(edge_rows, "lon", lax.axis_size("lon") // 2)
    band_index = lax.axis_index("lat")
    northern = band_index == 0
    southern = band_index == lax.axis_size("lat") - 1
    top_row = jnp.where(northern, across[:, :1], banded[:, :1])
    bottom_row = jnp.where(southern, across[:, 1:], banded[:, -1:])
    joined = jnp.concatenate([top_row, banded[:, 1:-1], bottom_row], axis=1)
    return with_halo(joined, (("lon", 2),), 1, True)


def windows(padded, row_count, col_count, flipped):
    result = []
    for position in range(9):
        lat_start = position // 3
        lon_start = position % 3
        if flipped:
            lat_start = 2 - lat_start
            lon_start = 2 - lon_start
        result.append(
            padded[:, lat_start : lat_start + row_count, lon_start : lon_start + col_count]
        )
    return result


def body(
    inputs_below,
    hidden_prev,
    cell_prev,
    kernel_weights,
    gate_bias,
    readout,
    target_field,
    land_mask,
    fire_mask,
    hidden_grad,
):
    hidden_width = hidden_prev.shape[0]
    input_width = inputs_below.shape[0]
    gate_count = kernel_weights.shape[1]
    channels = kernel_weights.shape[2]
    row_count = cell_prev.shape[1]
    col_count = cell_prev.shape[2]
    stacked = jnp.concatenate([inputs_below, hidden_prev], axis=0)
    padded = extend(stacked)
    forward_windows = windows(padded, row_count, col_count, False)
    preact = jnp.zeros((gate_count, row_count, col_count), jnp.float32)
    for position in range(9):
        preact = preact + jnp.einsum(
            "gc,crw->grw",
            kernel_weights[position],
            forward_windows[position],
            preferred_element_type=jnp.float32,
        )
    preact = preact + gate_bias[:, None, None]
    input_gate = jax.nn.sigmoid(preact[0:hidden_width])
    forget_gate = jax.nn.sigmoid(preact[hidden_width : 2 * hidden_width])
    output_gate = jax.nn.sigmoid(preact[2 * hidden_width : 3 * hidden_width])
    candidate = jnp.tanh(preact[3 * hidden_width : 4 * hidden_width])
    land_float = land_mask.astype(jnp.float32)[None]
    fire_float = fire_mask.astype(jnp.float32)
    cell_next = land_float * (forget_gate * cell_prev + input_gate * candidate)
    squashed = jnp.tanh(cell_next)
    hidden_next = (output_gate * squashed).astype(jnp.bfloat16)
    predicted = jnp.sum(readout[:, None, None] * hidden_next.astype(jnp.float32), axis=0)
    total_grad = (
        hidden_grad.astype(jnp.float32)
        + 2.0 * (fire_float * (predicted - target_field))[None] * readout[:, None, None]
    )
    cell_grad = land_float * total_grad * output_gate * (1.0 - squashed * squashed)
    grad_cell = cell_grad * forget_gate
    pre_grad = jnp.concatenate(
        [
            cell_grad * candidate * input_gate * (1.0 - input_gate),
            cell_grad * cell_prev * forget_gate * (1.0 - forget_gate),
            total_grad * squashed * output_gate * (1.0 - output_gate),
            cell_grad * input_gate * (1.0 - candidate * candidate),
        ],
        axis=0,
    )
    pre_low = pre_grad.astype(jnp.bfloat16)
    local_bias = jnp.sum(pre_grad, axis=(1, 2))
    local_kernel = jnp.stack(
        [
            jnp.einsum(
                "grw,crw->gc",
                pre_low,
                forward_windows[position],
                preferred_element_type=jnp.float32,
            )
            for position in range(9)
        ],
        axis=0,
    )
    grad_padded = extend(pre_low)
    band_index = lax.axis_index("lat")
    northern = band_index == 0
    southern = band_index == lax.axis_size("lat") - 1
    row_index = lax.broadcasted_iota(jnp.int32, (1, row_count + 2, 1), 1)
    pole_rows = northern & (row_index == 0) | southern & (row_index == row_count + 1)
    main_padded = jnp.where(pole_rows, jnp.zeros_like(grad_padded), grad_padded)
    back_windows = windows(main_padded, row_count, col_count, True)
    field_grad = jnp.zeros((channels, row_count, col_count), jnp.float32)
    for position in range(9):
        field_grad = field_grad + jnp.einsum(
            "gc,grw->crw",
            kernel_weights[position],
            back_windows[position],
            preferred_element_type=jnp.float32,
        )
    north_term = jnp.zeros((channels, col_count), jnp.float32)
    south_term = jnp.zeros((channels, col_count), jnp.float32)
    for position in range(3):
        lon_start = 2 - position
        north_term = north_term + jnp.einsum(
            "gc,gw->cw",
            kernel_weights[position],
            grad_padded[:, 0, lon_start : lon_start + col_count],
            preferred_element_type=jnp.float32,
        )
        south_term = south_term + jnp.einsum(
            "gc,gw->cw",
            kernel_weights[6 + position],
            grad_padded[:, row_count + 1, lon_start : lon_start + col_count],
            preferred_element_type=jnp.float32,
        )
    field_grad = field_grad.at[:, 0].add(jnp.where(northern, north_term, 0.0))
    field_grad = field_grad.at[:, row_count - 1].add(jnp.where(southern, south_term, 0.0))
    grad_inputs = field_grad[:input_width].astype(jnp.bfloat16)
    grad_hidden = field_grad[input_width:].astype(jnp.bfloat16)
    scaling = 1.0 / math.sqrt(row_count * lax.axis_size("lat") * col_count * lax.axis_size("lon"))
    summed_kernel, summed_bias = lax.psum((local_kernel, local_bias), ("lat", "lon"))
    grad_kernel = summed_kernel * scaling
    grad_bias = summed_bias * scaling
    return (hidden_next, cell_next, grad_inputs, grad_hidden, grad_cell, grad_kernel, grad_bias)


def solution(mesh):
    return jax.shard_map(
        body,
        mesh=mesh,
        in_specs=(
            P(None, "lat", "lon"),
            P(None, "lat", "lon"),
            P(None, "lat", "lon"),
            P(),
            P(),
            P(),
            P("lat", "lon"),
            P("lat", "lon"),
            P("lat", "lon"),
            P(None, "lat", "lon"),
        ),
        out_specs=(
            P(None, "lat", "lon"),
            P(None, "lat", "lon"),
            P(None, "lat", "lon"),
            P(None, "lat", "lon"),
            P(None, "lat", "lon"),
            P(),
            P(),
        ),
        check_vma=False,
    )
```

profile of v0, /device:TPU:1, one launch (start us, length us, event | category | flops | bytes accessed | tf_op | source)
XLA Modules:
  0.0 486.5 jit_solution(17038042296153973256)
XLA Ops:
  7.2 1.1 copy.215
  8.4 1.1 copy.216
  9.6 12.0 %collective-permute-start.1 = (bf16[128,1,128]{0,2,1:T(8,128)(2,1)S(1)}, bf16[128,1,128]{0,2,1:T(8,128)(2,1)S(1)}, u32[]{:S(2)}, u32[]{:S(2)}) collective-permute-start(bf16[128,1,128]{0,2,1:T(8,128)(2,1)S(1)} %get-tuple-element.98), channel_id=1, source_target_pairs={{0,32},{32,64},{64,96},{96,128},{128,160},{160,192},{192,224},{224... | collective-permute-start | bytes 98312 | tf_op jit(solution)/shard_map/ppermute | solution.py:16
  21.6 1.9 collective-permute-start.2
  23.6 7.5 %collective-permute-start = (bf16[128,2,128]{0,2,1:T(8,128)(2,1)S(1)}, bf16[128,2,128]{0,2,1:T(8,128)(2,1)S(1)}, u32[]{:S(2)}, u32[]{:S(2)}) collective-permute-start(bf16[128,2,128]{0,2,1:T(8,128)(2,1)S(1)} %pad_maximum_fusion.13), channel_id=1, source_target_pairs={{0,16},{1,17},{2,18},{3,19},{4,20},{5,21},{6,22},{7,23},{8,24},{9,... | collective-permute-start | bytes 196616 | tf_op jit(solution)/shard_map/ppermute | solution.py:28
  31.0 0.3 fusion.105
  31.4 1.3 copy.221
  32.8 0.3 fusion.30
  33.2 3.1 collective-permute-start.3
  36.3 7.1 %collective-permute-start.4 = (bf16[128,10,1]{0,2,1:T(2,128)(2,1)S(1)}, bf16[128,10,1]{0,2,1:T(2,128)(2,1)S(1)}, u32[]{:S(2)}, u32[]{:S(2)}) collective-permute-start(bf16[128,10,1]{0,2,1:T(2,128)(2,1)S(1)} %get-tuple-element.95), channel_id=1, source_target_pairs={{1,0},{2,1},{3,2},{4,3},{5,4},{6,5},{7,6},{8,7},{9,8},{10,9},{11,1... | collective-permute-start | bytes 7688 | tf_op jit(solution)/shard_map/ppermute | solution.py:18
  43.4 0.4 fusion.36
  43.8 1.3 copy.218
  45.1 1.3 copy.224
  46.4 0.3 maximum_maximum_fusion
  46.8 1.3 fusion.77
  48.1 0.3 fusion.71
  48.4 1.3 fusion.74
  49.6 1.4 fusion.68
  51.0 1.3 fusion.65
  52.3 0.3 fusion.62
  52.6 2.5 copy.217
  55.1 2.6 copy.219
  57.7 1.3 copy.220
  59.0 2.6 copy.222
  61.6 1.4 copy.223
  63.1 1.3 copy.225
  64.4 3.9 add_bitcast_fusion
  68.3 1.0 multiply_reduce_fusion
  69.3 0.9 fusion.157
  70.6 0.9 copy-done.7
  71.5 0.9 fusion.9
  72.6 9.0 %collective-permute-start.6 = (bf16[256,1,128]{2,1,0:T(2,128)(2,1)S(1)}, bf16[256,1,128]{2,1,0:T(2,128)(2,1)S(1)}, u32[]{:S(2)}, u32[]{:S(2)}) collective-permute-start(bf16[256,1,128]{2,1,0:T(2,128)(2,1)S(1)} %get-tuple-element.96), channel_id=1, source_target_pairs={{0,32},{32,64},{64,96},{96,128},{128,160},{160,192},{192,224},{224... | collective-permute-start | bytes 196616 | tf_op jit(solution)/shard_map/ppermute | solution.py:16
  81.6 0.3 pad_maximum_fusion.12
  81.9 1.9 collective-permute-start.7
  83.8 1.0 fusion.8
  84.8 1.0 fusion.7
  85.8 0.9 fusion.6
  86.7 1.0 fusion.5
  87.8 1.0 fusion.4
  88.8 0.9 fusion.3
  89.7 1.0 fusion.2
  90.8 7.1 %collective-permute-start.5 = (bf16[256,2,128]{2,1,0:T(2,128)(2,1)S(1)}, bf16[256,2,128]{2,1,0:T(2,128)(2,1)S(1)}, u32[]{:S(2)}, u32[]{:S(2)}) collective-permute-start(bf16[256,2,128]{2,1,0:T(2,128)(2,1)S(1)} %pad_maximum_fusion.12), channel_id=1, source_target_pairs={{0,16},{1,17},{2,18},{3,19},{4,20},{5,21},{6,22},{7,23},{8,24},{9,... | collective-permute-start | bytes 393224 | tf_op jit(solution)/shard_map/ppermute | solution.py:28
  97.9 1.0 fusion.1
  98.9 1.0 fusion.18
  99.9 98.2 %psum.15 = f32[256]{0:T(256)S(1)} all-reduce(f32[256]{0:T(256)S(1)} %fusion.18), channel_id=1, replica_groups=mesh['lat'=16,'lon'=32] {'lat','lon'}, use_global_device_ids=true, to_apply=%region_3.4 | all-reduce | flops 256 | bytes 2048 | tf_op jit(solution)/shard_map/psum | solution.py:164
  198.1 0.4 broadcast_select_fusion.1
  198.5 0.6 pad_maximum_fusion.1
  199.2 0.5 fusion.159
  199.6 0.9 copy.226
  200.5 3.2 collective-permute-start.8
  203.8 0.9 copy.227
  204.7 5.9 %collective-permute-start.9 = (bf16[256,10,1]{0,1,2:T(8,128)(2,1)S(1)}, bf16[256,10,1]{0,1,2:T(8,128)(2,1)S(1)}, u32[]{:S(2)}, u32[]{:S(2)}) collective-permute-start(bf16[256,10,1]{0,1,2:T(8,128)(2,1)S(1)} %copy.227), channel_id=1, source_target_pairs={{1,0},{2,1},{3,2},{4,3},{5,4},{6,5},{7,6},{8,7},{9,8},{10,9},{11,1... | collective-permute-start | bytes 15368 | tf_op jit(solution)/shard_map/ppermute | solution.py:18
  210.6 0.6 broadcast_multiply_fusion.1
  211.2 1.0 copy.228
  212.3 1.0 copy.229
  213.3 1.5 pad_maximum_fusion.4
  215.5 2.7 maximum_select_fusion
  218.2 1.4 fusion.158
  221.0 0.3 convolution_add_fusion.3
  221.3 0.3 convolution_add_fusion.2
  222.9 0.7 copy.268
  223.6 0.7 copy.269
  224.4 252.9 %all-reduce.2.cloned.1.call-done = f32[9,256,128]{2,1,0:T(8,128)} async-done(((f32[9,256,128]{2,1,0:T(8,128)}), f32[9,256,128]{2,1,0:T(8,128)}) %all-reduce.2.cloned.1.call-update) | async-done | bytes 1179664 | tf_op jit(solution)/shard_map/psum | solution.py:164
  477.3 2.4 broadcast_multiply_fusion
  (68 shorter events, 4.1 us)
Async XLA Ops:
  7.2 23.9 %copy-start.1 = (bf16[9,256,128]{2,1,0:T(8,128)(2,1)S(1)}, bf16[9,256,128]{2,1,0:T(8,128)(2,1)}, u32[]{:S(2)}) copy-start(bf16[9,256,128]{2,1,0:T(8,128)(2,1)} %param.17) | copy-start | bytes 1769476
  7.2 470.1 %all-reduce.2.cloned.1.call-start = ((), (), s32[]{:S(2)}) async-start(), calls=%async_computation | async-start | bytes 2359296 | tf_op jit(solution)/shard_map/psum | solution.py:164
  9.6 23.2 %collective-permute-start.1 = (bf16[128,1,128]{0,2,1:T(8,128)(2,1)S(1)}, bf16[128,1,128]{0,2,1:T(8,128)(2,1)S(1)}, u32[]{:S(2)}, u32[]{:S(2)}) collective-permute-start(bf16[128,1,128]{0,2,1:T(8,128)(2,1)S(1)} %get-tuple-element.98), channel_id=1, source_target_pairs={{0,32},{32,64},{64,96},{96,128},{128,160},{160,192},{192,224},{224... | collective-permute-start | bytes 98312 | tf_op jit(solution)/shard_map/ppermute | solution.py:16
  21.6 11.1 %collective-permute-start.2 = (bf16[128,1,128]{0,2,1:T(8,128)(2,1)S(1)}, bf16[128,1,128]{0,2,1:T(8,128)(2,1)S(1)}, u32[]{:S(2)}, u32[]{:S(2)}) collective-permute-start(bf16[128,1,128]{0,2,1:T(8,128)(2,1)S(1)} %get-tuple-element.99), channel_id=1, source_target_pairs={{32,0},{64,32},{96,64},{128,96},{160,128},{192,160},{224,192},{256... | collective-permute-start | bytes 98312 | tf_op jit(solution)/shard_map/ppermute | solution.py:18
  23.6 9.2 %collective-permute-start = (bf16[128,2,128]{0,2,1:T(8,128)(2,1)S(1)}, bf16[128,2,128]{0,2,1:T(8,128)(2,1)S(1)}, u32[]{:S(2)}, u32[]{:S(2)}) collective-permute-start(bf16[128,2,128]{0,2,1:T(8,128)(2,1)S(1)} %pad_maximum_fusion.13), channel_id=1, source_target_pairs={{0,16},{1,17},{2,18},{3,19},{4,20},{5,21},{6,22},{7,23},{8,24},{9,... | collective-permute-start | bytes 196616 | tf_op jit(solution)/shard_map/ppermute | solution.py:28
  31.4 1.3 copy-start.11
  33.2 13.2 %collective-permute-start.3 = (bf16[128,10,1]{0,2,1:T(2,128)(2,1)S(1)}, bf16[128,10,1]{0,2,1:T(2,128)(2,1)S(1)}, u32[]{:S(2)}, u32[]{:S(2)}) collective-permute-start(bf16[128,10,1]{0,2,1:T(2,128)(2,1)S(1)} %get-tuple-element.94), channel_id=1, source_target_pairs={{0,1},{1,2},{2,3},{3,4},{4,5},{5,6},{6,7},{7,8},{8,9},{9,10},{10,1... | collective-permute-start | bytes 7688 | tf_op jit(solution)/shard_map/ppermute | solution.py:16
  36.3 10.1 %collective-permute-start.4 = (bf16[128,10,1]{0,2,1:T(2,128)(2,1)S(1)}, bf16[128,10,1]{0,2,1:T(2,128)(2,1)S(1)}, u32[]{:S(2)}, u32[]{:S(2)}) collective-permute-start(bf16[128,10,1]{0,2,1:T(2,128)(2,1)S(1)} %get-tuple-element.95), channel_id=1, source_target_pairs={{1,0},{2,1},{3,2},{4,3},{5,4},{6,5},{7,6},{8,7},{9,8},{10,9},{11,1... | collective-permute-start | bytes 7688 | tf_op jit(solution)/shard_map/ppermute | solution.py:18
  46.8 4.3 copy-start.6
  46.8 5.5 %copy-start.4 = (bf16[128,10,129]{0,2,1:T(8,128)(2,1)}, bf16[128,10,129]{0,2,1:T(8,128)(2,1)S(1)}, u32[]{:S(2)}) copy-start(bf16[128,10,129]{0,2,1:T(8,128)(2,1)S(1)} %get-tuple-element.93) | copy-start | bytes 990724
  59.0 2.6 copy-start
  63.1 1.3 copy-start.3
  63.1 1.3 copy-start.15
  64.4 3.9 copy-start.9
  64.4 3.9 copy-start.14
  68.3 1.0 copy-start.12
  68.3 1.0 copy-start.13
  68.3 1.0 copy-start.10
  69.3 1.2 copy-start.8
  70.5 1.0 copy-start.7
  72.4 12.4 %copy-start.5 = (bf16[128,10,129]{0,2,1:T(8,128)(2,1)S(1)}, bf16[128,10,129]{0,2,1:T(8,128)(2,1)}, u32[]{:S(2)}) copy-start(bf16[128,10,129]{0,2,1:T(8,128)(2,1)} %copy-done.4) | copy-start | bytes 990724
  72.6 125.5 %collective-permute-start.6 = (bf16[256,1,128]{2,1,0:T(2,128)(2,1)S(1)}, bf16[256,1,128]{2,1,0:T(2,128)(2,1)S(1)}, u32[]{:S(2)}, u32[]{:S(2)}) collective-permute-start(bf16[256,1,128]{2,1,0:T(2,128)(2,1)S(1)} %get-tuple-element.96), channel_id=1, source_target_pairs={{0,32},{32,64},{64,96},{96,128},{128,160},{160,192},{192,224},{224... | collective-permute-start | bytes 196616 | tf_op jit(solution)/shard_map/ppermute | solution.py:16
  81.9 116.2 %collective-permute-start.7 = (bf16[256,1,128]{2,1,0:T(2,128)(2,1)S(1)}, bf16[256,1,128]{2,1,0:T(2,128)(2,1)S(1)}, u32[]{:S(2)}, u32[]{:S(2)}) collective-permute-start(bf16[256,1,128]{2,1,0:T(2,128)(2,1)S(1)} %get-tuple-element.97), channel_id=1, source_target_pairs={{32,0},{64,32},{96,64},{128,96},{160,128},{192,160},{224,192},{256... | collective-permute-start | bytes 196616 | tf_op jit(solution)/shard_map/ppermute | solution.py:18
  90.8 107.3 %collective-permute-start.5 = (bf16[256,2,128]{2,1,0:T(2,128)(2,1)S(1)}, bf16[256,2,128]{2,1,0:T(2,128)(2,1)S(1)}, u32[]{:S(2)}, u32[]{:S(2)}) collective-permute-start(bf16[256,2,128]{2,1,0:T(2,128)(2,1)S(1)} %pad_maximum_fusion.12), channel_id=1, source_target_pairs={{0,16},{1,17},{2,18},{3,19},{4,20},{5,21},{6,22},{7,23},{8,24},{9,... | collective-permute-start | bytes 393224 | tf_op jit(solution)/shard_map/ppermute | solution.py:28
  200.5 10.7 %collective-permute-start.8 = (bf16[256,10,1]{0,1,2:T(8,128)(2,1)S(1)}, bf16[256,10,1]{0,1,2:T(8,128)(2,1)S(1)}, u32[]{:S(2)}, u32[]{:S(2)}) collective-permute-start(bf16[256,10,1]{0,1,2:T(8,128)(2,1)S(1)} %copy.226), channel_id=1, source_target_pairs={{0,1},{1,2},{2,3},{3,4},{4,5},{5,6},{6,7},{7,8},{8,9},{9,10},{10,1... | collective-permute-start | bytes 15368 | tf_op jit(solution)/shard_map/ppermute | solution.py:16
  204.7 7.6 %collective-permute-start.9 = (bf16[256,10,1]{0,1,2:T(8,128)(2,1)S(1)}, bf16[256,10,1]{0,1,2:T(8,128)(2,1)S(1)}, u32[]{:S(2)}, u32[]{:S(2)}) collective-permute-start(bf16[256,10,1]{0,1,2:T(8,128)(2,1)S(1)} %copy.227), channel_id=1, source_target_pairs={{1,0},{2,1},{3,2},{4,3},{5,4},{6,5},{7,6},{8,7},{9,8},{10,9},{11,1... | collective-permute-start | bytes 15368 | tf_op jit(solution)/shard_map/ppermute | solution.py:18
  213.3 1.6 copy-start.2
Sparse Core Ops, SparseCore 0:
  211.3 265.8 all-reduce.1
where the time goes:
time: 487 us; the launch traced here: 486 us
  waiting for transfers between devices  253 us (52%)
  blocking collectives  98.2 us (20%)
  starting transfers between devices  58.8 us (12%)
  local copies, waits for them, and re-layouts  26.3 us (5%)
  matrix products  19.5 us (4%)
  other arithmetic  16.2 us (3%)
  between operations  14.6 us (3%)
    psum x1, waiting for transfers between devices, body(): lax.psum((local_kernel, local_bias), ('lat', 'lon'))  253 us
    psum x1, blocking collectives, body(): lax.psum((local_kernel, local_bias), ('lat', 'lon'))  98.2 us
    ppermute x4, starting transfers between devices, with_halo(): lax.ppermute(tail, axis, [(i, (i + 1) % count) for i in range(ends)])  27.3 us
    ppermute x4, starting transfers between devices, with_halo(): lax.ppermute(head, axis, [((i + 1) % count, i) for i in range(ends)])  16.8 us
    dot_general x9, local copies, waits for them, and re-layouts, body(): jnp.einsum('gc,crw->grw', kernel_weights[position], forward_windows[posit...  15.7 us
    ppermute x2, starting transfers between devices, shifted(): return lax.ppermute(value, axis, pairs)  14.6 us
  transfers between devices with their start and end apart: 11, of which 1 were waited for; matrix products, arithmetic and copies ran while one was open for 6% of the time, Pallas kernels for 0%

commit v1 on v0

--- a/solution.py
+++ b/solution.py
@@ -3,6 +3,12 @@
 import jax.numpy as jnp
 from jax import lax
 from jax.sharding import PartitionSpec as P
+
+
+def fit_bars(xs, axis_id, ax_name):
+    for c in (axis_id, ax_name):
+        xs = jax.lax.psum(xs, axis_name=c)
+    return xs
 
 
 def with_halo(cells, sides, width, closed):
@@ -161,7 +167,7 @@
     grad_inputs = field_grad[:input_width].astype(jnp.bfloat16)
     grad_hidden = field_grad[input_width:].astype(jnp.bfloat16)
     scaling = 1.0 / math.sqrt(row_count * lax.axis_size("lat") * col_count * lax.axis_size("lon"))
-    summed_kernel, summed_bias = lax.psum((local_kernel, local_bias), ("lat", "lon"))
+    summed_kernel, summed_bias = fit_bars((local_kernel, local_bias), "lon", ax_name="lat")
     grad_kernel = summed_kernel * scaling
     grad_bias = summed_bias * scaling
     return (hidden_next, cell_next, grad_inputs, grad_hidden, grad_cell, grad_kernel, grad_bias)

time: 487 us -> 734 us (1.51)
  waiting for transfers between devices: 253 us -> 472 us
  blocking collectives: 98.2 us -> 122 us
    psum x1 -> x2, waiting for transfers between devices: 253 us -> 472 us  [fit_bars(): xs = jax.lax.psum(xs, axis_name=c)]
    psum x1 -> x2, blocking collectives: 98.2 us -> 122 us  [fit_bars(): xs = jax.lax.psum(xs, axis_name=c)]
  transfers between devices with their start and end apart: 11 -> 12, of which waited for: 1 -> 2; matrix products, arithmetic and copies ran while one was open for 6% -> 4% of each run, Pallas kernels for 0% -> 0%
where the time goes in v1:
time: 734 us; the launch traced here: 733 us
  waiting for transfers between devices  472 us (64%)
  blocking collectives  122 us (17%)
  starting transfers between devices  58.9 us (8%)
  local copies, waits for them, and re-layouts  26.3 us (4%)
  matrix products  22.8 us (3%)
  other arithmetic  16.2 us (2%)
  between operations  14.6 us (2%)
    psum x2, waiting for transfers between devices, fit_bars(): xs = jax.lax.psum(xs, axis_name=c)  472 us
    psum x2, blocking collectives, fit_bars(): xs = jax.lax.psum(xs, axis_name=c)  122 us
    ppermute x4, starting transfers between devices, with_halo(): lax.ppermute(tail, axis, [(i, (i + 1) % count) for i in range(ends)])  26 us
    ppermute x4, starting transfers between devices, with_halo(): lax.ppermute(head, axis, [((i + 1) % count, i) for i in range(ends)])  18.2 us
    dot_general x9, local copies, waits for them, and re-layouts, body(): jnp.einsum('gc,crw->grw', kernel_weights[position], forward_windows[posit...  15.7 us
  transfers between devices with their start and end apart: 12, of which 2 were waited for; matrix products, arithmetic and copies ran while one was open for 4% of the time, Pallas kernels for 0%

profile of v1, /device:TPU:1, one launch (start us, length us, event | category | flops | bytes accessed | tf_op | source)
XLA Modules:
  0.0 733.2 jit_solution(12321015469565326538)
XLA Ops:
  7.2 1.1 copy.215
  8.4 1.1 copy.216
  9.6 12.0 %collective-permute-start.1 = (bf16[128,1,128]{0,2,1:T(8,128)(2,1)S(1)}, bf16[128,1,128]{0,2,1:T(8,128)(2,1)S(1)}, u32[]{:S(2)}, u32[]{:S(2)}) collective-permute-start(bf16[128,1,128]{0,2,1:T(8,128)(2,1)S(1)} %get-tuple-element.98), channel_id=1, source_target_pairs={{0,32},{32,64},{64,96},{96,128},{128,160},{160,192},{192,224},{224... | collective-permute-start | bytes 98312 | tf_op jit(solution)/shard_map/ppermute | solution.py:22
  21.6 1.9 collective-permute-start.2
  23.6 7.5 %collective-permute-start = (bf16[128,2,128]{0,2,1:T(8,128)(2,1)S(1)}, bf16[128,2,128]{0,2,1:T(8,128)(2,1)S(1)}, u32[]{:S(2)}, u32[]{:S(2)}) collective-permute-start(bf16[128,2,128]{0,2,1:T(8,128)(2,1)S(1)} %pad_maximum_fusion.13), channel_id=1, source_target_pairs={{0,16},{1,17},{2,18},{3,19},{4,20},{5,21},{6,22},{7,23},{8,24},{9,... | collective-permute-start | bytes 196616 | tf_op jit(solution)/shard_map/ppermute | solution.py:34
  31.0 0.3 fusion.105
  31.4 1.3 copy.221
  32.8 0.3 fusion.30
  33.2 3.1 collective-permute-start.3
  36.3 7.1 collective-permute-start.4
  43.4 0.4 fusion.36
  43.8 1.3 copy.218
  45.1 1.4 copy.224
  46.8 1.3 fusion.77
  48.4 1.3 fusion.74
  49.7 1.4 fusion.68
  51.1 1.3 fusion.65
  52.6 2.5 copy.217
  55.2 2.6 copy.219
  57.7 1.3 copy.220
  59.1 2.6 copy.222
  61.7 1.4 copy.223
  63.1 1.3 copy.225
  64.4 3.9 add_bitcast_fusion
  68.4 1.0 multiply_reduce_fusion
  69.4 0.9 fusion.157
  70.6 0.9 copy-done.7
  71.5 0.9 fusion.9
  72.6 9.0 %collective-permute-start.6 = (bf16[256,1,128]{2,1,0:T(2,128)(2,1)S(1)}, bf16[256,1,128]{2,1,0:T(2,128)(2,1)S(1)}, u32[]{:S(2)}, u32[]{:S(2)}) collective-permute-start(bf16[256,1,128]{2,1,0:T(2,128)(2,1)S(1)} %get-tuple-element.96), channel_id=1, source_target_pairs={{0,32},{32,64},{64,96},{96,128},{128,160},{160,192},{192,224},{224... | collective-permute-start | bytes 196616 | tf_op jit(solution)/shard_map/ppermute | solution.py:22
  81.9 1.9 collective-permute-start.7
  83.8 1.0 fusion.8
  84.9 1.0 fusion.7
  85.8 0.9 fusion.6
  86.8 1.0 fusion.5
  87.8 1.0 fusion.4
  88.8 0.9 fusion.3
  89.8 1.0 fusion.2
  90.8 7.1 collective-permute-start.5
  98.0 1.0 fusion.1
  98.9 1.0 fusion.18
  100.0 64.7 %psum.30 = f32[256]{0:T(256)S(1)} all-reduce(f32[256]{0:T(256)S(1)} %fusion.18), channel_id=1, replica_groups=mesh['lat'=16,'lon'=32] {'lon'}, use_global_device_ids=true, to_apply=%region_4.5 | all-reduce | flops 256 | bytes 2048 | tf_op jit(solution)/shard_map/psum | solution.py:10
  164.6 57.2 %psum.31 = f32[256]{0:T(256)S(1)} all-reduce(f32[256]{0:T(256)S(1)} %psum.30), channel_id=1, replica_groups=mesh['lat'=16,'lon'=32] {'lat'}, use_global_device_ids=true, to_apply=%region_5.6 | all-reduce | flops 256 | bytes 2048 | tf_op jit(solution)/shard_map/psum | solution.py:10
  221.9 0.4 broadcast_select_fusion.1
  222.3 0.6 pad_maximum_fusion.1
  222.9 0.5 fusion.159
  223.4 0.9 copy.226
  224.3 1.9 collective-permute-start.8
  226.2 0.9 copy.227
  227.1 7.3 collective-permute-start.9
  234.4 0.6 broadcast_multiply_fusion.1
  235.1 1.0 copy.228
  236.1 1.0 copy.229
  237.1 1.5 pad_maximum_fusion.4
  239.1 2.7 maximum_select_fusion
  241.8 1.4 fusion.158
  245.7 264.5 %all-reduce.3.cloned.1.call-done = f32[9,256,128]{2,1,0:T(8,128)} async-done(((f32[9,256,128]{2,1,0:T(8,128)}), f32[9,256,128]{2,1,0:T(8,128)}) %all-reduce.3.cloned.1.call-update) | async-done | bytes 1179664 | tf_op jit(solution)/shard_map/psum | solution.py:10
  510.2 1.1 convolution_add_fusion.11
  511.2 1.1 fusion
  512.4 1.1 fusion.15
  513.4 1.1 fusion.17
  514.6 0.7 copy.268
  515.3 0.7 copy.269
  516.1 207.9 %all-reduce.5.cloned.1.call-done = f32[9,256,128]{2,1,0:T(8,128)} async-done(((f32[9,256,128]{2,1,0:T(8,128)}), f32[9,256,128]{2,1,0:T(8,128)}) %all-reduce.5.cloned.1.call-update) | async-done | bytes 1179664 | tf_op jit(solution)/shard_map/psum | solution.py:10
  724.0 2.4 broadcast_multiply_fusion
  (72 shorter events, 5.0 us)
Async XLA Ops:
  7.2 23.9 %copy-start.1 = (bf16[9,256,128]{2,1,0:T(8,128)(2,1)S(1)}, bf16[9,256,128]{2,1,0:T(8,128)(2,1)}, u32[]{:S(2)}) copy-start(bf16[9,256,128]{2,1,0:T(8,128)(2,1)} %param.17) | copy-start | bytes 1769476
  7.2 503.0 %all-reduce.3.cloned.1.call-start = ((), (), s32[]{:S(2)}) async-start(), calls=%async_computation | async-start | bytes 2359296 | tf_op jit(solution)/shard_map/psum | solution.py:10
  9.6 23.1 %collective-permute-start.1 = (bf16[128,1,128]{0,2,1:T(8,128)(2,1)S(1)}, bf16[128,1,128]{0,2,1:T(8,128)(2,1)S(1)}, u32[]{:S(2)}, u32[]{:S(2)}) collective-permute-start(bf16[128,1,128]{0,2,1:T(8,128)(2,1)S(1)} %get-tuple-element.98), channel_id=1, source_target_pairs={{0,32},{32,64},{64,96},{96,128},{128,160},{160,192},{192,224},{224... | collective-permute-start | bytes 98312 | tf_op jit(solution)/shard_map/ppermute | solution.py:22
  21.6 11.1 %collective-permute-start.2 = (bf16[128,1,128]{0,2,1:T(8,128)(2,1)S(1)}, bf16[128,1,128]{0,2,1:T(8,128)(2,1)S(1)}, u32[]{:S(2)}, u32[]{:S(2)}) collective-permute-start(bf16[128,1,128]{0,2,1:T(8,128)(2,1)S(1)} %get-tuple-element.99), channel_id=1, source_target_pairs={{32,0},{64,32},{96,64},{128,96},{160,128},{192,160},{224,192},{256... | collective-permute-start | bytes 98312 | tf_op jit(solution)/shard_map/ppermute | solution.py:24
  23.6 9.2 %collective-permute-start = (bf16[128,2,128]{0,2,1:T(8,128)(2,1)S(1)}, bf16[128,2,128]{0,2,1:T(8,128)(2,1)S(1)}, u32[]{:S(2)}, u32[]{:S(2)}) collective-permute-start(bf16[128,2,128]{0,2,1:T(8,128)(2,1)S(1)} %pad_maximum_fusion.13), channel_id=1, source_target_pairs={{0,16},{1,17},{2,18},{3,19},{4,20},{5,21},{6,22},{7,23},{8,24},{9,... | collective-permute-start | bytes 196616 | tf_op jit(solution)/shard_map/ppermute | solution.py:34
  31.4 1.3 copy-start.11
  33.2 13.3 %collective-permute-start.3 = (bf16[128,10,1]{0,2,1:T(2,128)(2,1)S(1)}, bf16[128,10,1]{0,2,1:T(2,128)(2,1)S(1)}, u32[]{:S(2)}, u32[]{:S(2)}) collective-permute-start(bf16[128,10,1]{0,2,1:T(2,128)(2,1)S(1)} %get-tuple-element.94), channel_id=1, source_target_pairs={{0,1},{1,2},{2,3},{3,4},{4,5},{5,6},{6,7},{7,8},{8,9},{9,10},{10,1... | collective-permute-start | bytes 7688 | tf_op jit(solution)/shard_map/ppermute | solution.py:22
  36.3 10.1 %collective-permute-start.4 = (bf16[128,10,1]{0,2,1:T(2,128)(2,1)S(1)}, bf16[128,10,1]{0,2,1:T(2,128)(2,1)S(1)}, u32[]{:S(2)}, u32[]{:S(2)}) collective-permute-start(bf16[128,10,1]{0,2,1:T(2,128)(2,1)S(1)} %get-tuple-element.95), channel_id=1, source_target_pairs={{1,0},{2,1},{3,2},{4,3},{5,4},{6,5},{7,6},{8,7},{9,8},{10,9},{11,1... | collective-permute-start | bytes 7688 | tf_op jit(solution)/shard_map/ppermute | solution.py:24
  46.8 4.3 copy-start.6
  46.8 5.5 copy-start.4
  59.1 2.6 copy-start
  63.1 1.3 copy-start.3
  63.1 1.3 copy-start.15
  64.4 3.9 copy-start.9
  64.4 3.9 copy-start.14
  68.3 1.0 copy-start.12
  68.3 1.0 copy-start.13
  68.4 1.0 copy-start.10
  69.3 1.2 copy-start.8
  70.5 1.0 copy-start.7
  72.5 12.4 %copy-start.5 = (bf16[128,10,129]{0,2,1:T(8,128)(2,1)S(1)}, bf16[128,10,129]{0,2,1:T(8,128)(2,1)}, u32[]{:S(2)}) copy-start(bf16[128,10,129]{0,2,1:T(8,128)(2,1)} %copy-done.4) | copy-start | bytes 990724
  72.6 149.2 %collective-permute-start.6 = (bf16[256,1,128]{2,1,0:T(2,128)(2,1)S(1)}, bf16[256,1,128]{2,1,0:T(2,128)(2,1)S(1)}, u32[]{:S(2)}, u32[]{:S(2)}) collective-permute-start(bf16[256,1,128]{2,1,0:T(2,128)(2,1)S(1)} %get-tuple-element.96), channel_id=1, source_target_pairs={{0,32},{32,64},{64,96},{96,128},{128,160},{160,192},{192,224},{224... | collective-permute-start | bytes 196616 | tf_op jit(solution)/shard_map/ppermute | solution.py:22
  81.9 140.0 %collective-permute-start.7 = (bf16[256,1,128]{2,1,0:T(2,128)(2,1)S(1)}, bf16[256,1,128]{2,1,0:T(2,128)(2,1)S(1)}, u32[]{:S(2)}, u32[]{:S(2)}) collective-permute-start(bf16[256,1,128]{2,1,0:T(2,128)(2,1)S(1)} %get-tuple-element.97), channel_id=1, source_target_pairs={{32,0},{64,32},{96,64},{128,96},{160,128},{192,160},{224,192},{256... | collective-permute-start | bytes 196616 | tf_op jit(solution)/shard_map/ppermute | solution.py:24
  90.8 131.1 %collective-permute-start.5 = (bf16[256,2,128]{2,1,0:T(2,128)(2,1)S(1)}, bf16[256,2,128]{2,1,0:T(2,128)(2,1)S(1)}, u32[]{:S(2)}, u32[]{:S(2)}) collective-permute-start(bf16[256,2,128]{2,1,0:T(2,128)(2,1)S(1)} %pad_maximum_fusion.12), channel_id=1, source_target_pairs={{0,16},{1,17},{2,18},{3,19},{4,20},{5,21},{6,22},{7,23},{8,24},{9,... | collective-permute-start | bytes 393224 | tf_op jit(solution)/shard_map/ppermute | solution.py:34
  224.3 10.7 %collective-permute-start.8 = (bf16[256,10,1]{0,1,2:T(8,128)(2,1)S(1)}, bf16[256,10,1]{0,1,2:T(8,128)(2,1)S(1)}, u32[]{:S(2)}, u32[]{:S(2)}) collective-permute-start(bf16[256,10,1]{0,1,2:T(8,128)(2,1)S(1)} %copy.226), channel_id=1, source_target_pairs={{0,1},{1,2},{2,3},{3,4},{4,5},{5,6},{6,7},{7,8},{8,9},{9,10},{10,1... | collective-permute-start | bytes 15368 | tf_op jit(solution)/shard_map/ppermute | solution.py:22
  227.1 8.9 %collective-permute-start.9 = (bf16[256,10,1]{0,1,2:T(8,128)(2,1)S(1)}, bf16[256,10,1]{0,1,2:T(8,128)(2,1)S(1)}, u32[]{:S(2)}, u32[]{:S(2)}) collective-permute-start(bf16[256,10,1]{0,1,2:T(8,128)(2,1)S(1)} %copy.227), channel_id=1, source_target_pairs={{1,0},{2,1},{3,2},{4,3},{5,4},{6,5},{7,6},{8,7},{9,8},{10,9},{11,1... | collective-permute-start | bytes 15368 | tf_op jit(solution)/shard_map/ppermute | solution.py:24
  235.0 489.0 %all-reduce.5.cloned.1.call-start = ((), (), s32[]{:S(2)}) async-start(), calls=%async_computation.1 | async-start | bytes 2359296 | tf_op jit(solution)/shard_map/psum | solution.py:10
  237.1 1.6 copy-start.2
Sparse Core Ops, SparseCore 0:
  235.1 274.9 all-reduce.2
  513.3 210.5 all-reduce.4
